TPU v7x, 32 devices: a whole 2x2x4 slice. The times are simulated.
32 devices in a mesh: dp: 8 (over y, x, core), mp: 4 (over z).
Axes of the slice: x: 2, y: 2, z: 4, core: 2. Of those that a mesh axis runs over, the one named last changes fastest.
Arguments:
- reservoir: bfloat16 [32768, 1024], P('dp'), may hold values from -6 to 6
- pull_list: int32 [8, 8, 1], P(None, 'dp'), may hold values from 0 to 31
- pull_counts: int32 [8, 8], P('dp'), may hold values from 0 to 1, as said below
- first_pattern: int32 [64, 2], P('mp'), may hold values from 0 to 7, all different within a row
- first_weight: bfloat16 [64, 2, 128, 128], P('mp'), may hold values from -0.375 to 0.375
- first_bias: float32 [8192], P('mp'), may hold values from -3 to 3
- second_pattern: int32 [64, 16], P('mp'), may hold values from 0 to 63, all different within a row
- second_weight: bfloat16 [64, 16, 128, 128], P('mp'), may hold values from -0.125 to 0.125
- cotangent: bfloat16 [4096, 8192], P('dp', 'mp'), may hold values from -0.09375 to 0.09375
Outputs:
- second_out: bfloat16 [4096, 8192], P('dp', 'mp')
- first_grad: float32 [64, 32768], P('mp', 'dp')
- second_grad: float32 [64, 262144], P('mp', 'dp')
- bias_grad: float32 [8192], P('mp')
Inputs may be any that keep to these rules, and one draw needn't show every extreme that they name: `pull_list`: only slots s below pull_counts[r, o] are used; others hold valid block numbers that are ignored. `pull_counts`: every row sums to 4; one owner gives 1 block to every requester.
All inputs are finite; a program needn't handle non-finite values.
Results may differ from a plain program's by a relative error of at most 0.019.
Values may be sent and summed in bfloat16 or wider, within the bound.
A program may use at most 128 MiB of HBM per device.

v0:
```python
import jax
import jax.numpy as jnp
from jax import lax
from jax.sharding import PartitionSpec as P


def silu_slope(v):
    s = jax.nn.sigmoid(v)
    return s * (1.0 + v * (1.0 - s))


def body(
    reservoir,
    pull_list,
    pull_counts,
    first_pattern,
    first_weight,
    first_bias,
    second_pattern,
    second_weight,
    cotangent,
):
    n_dp = lax.axis_size("dp")
    side = first_weight.shape[2]
    width_in = reservoir.shape[1]
    cap = pull_list.shape[2]
    rows_dev = cotangent.shape[0]
    blocks_dev = rows_dev // side
    local_cols = first_weight.shape[0]
    slots = n_dp * cap
    stored = reservoir.reshape(-1, side, width_in)
    picks = pull_list[:, 0, :]
    counts = pull_counts[0]
    position = jnp.arange(slots, dtype=jnp.int32)
    owner = position // cap
    within = position % cap
    prefix = jnp.cumsum(counts) - counts
    dest = jnp.where(within < counts[owner], prefix[owner] + within, -1)
    selector = (dest[None, :] == jnp.arange(blocks_dev, dtype=jnp.int32)[:, None]).astype(
        jnp.bfloat16
    )
    sending = stored[picks]
    received = lax.all_to_all(sending, "dp", split_axis=0, concat_axis=0, tiled=True)
    flat = received.reshape(slots, -1)
    inputs = (
        jnp.dot(selector, flat, preferred_element_type=jnp.float32)
        .astype(jnp.bfloat16)
        .reshape(rows_dev, width_in)
    )
    picked1 = inputs.reshape(rows_dev, width_in // side, side)[:, first_pattern]
    pre = jnp.einsum(
        "rckf,ckfg->rcg", picked1, first_weight, preferred_element_type=jnp.float32
    ) + first_bias.reshape(local_cols, side)
    hidden = jax.nn.silu(pre).astype(jnp.bfloat16).reshape(rows_dev, local_cols * side)
    whole_hidden = lax.all_gather(hidden, "mp", axis=1, tiled=True)
    all_blocks = whole_hidden.shape[1] // side
    picked2 = whole_hidden.reshape(rows_dev, all_blocks, side)[:, second_pattern]
    second_out = jnp.einsum(
        "rckf,ckfg->rcg", picked2, second_weight, preferred_element_type=jnp.float32
    ).astype(jnp.bfloat16)
    upstream = cotangent.reshape(rows_dev, local_cols, side)
    second_part = jnp.einsum(
        "rckf,rcg->ckfg", picked2, upstream, preferred_element_type=jnp.float32
    ).astype(jnp.bfloat16)

    def add_column(column, total):
        up_column = lax.dynamic_index_in_dim(upstream, column, 1, keepdims=False)
        weight_column = lax.dynamic_index_in_dim(second_weight, column, 0, keepdims=False)
        where = lax.dynamic_index_in_dim(second_pattern, column, 0, keepdims=False)
        spread = jnp.einsum(
            "rg,kfg->rkf", up_column, weight_column, preferred_element_type=jnp.float32
        )
        return total.at[:, where].add(spread)

    term = lax.fori_loop(
        0, local_cols, add_column, jnp.zeros((rows_dev, all_blocks, side), jnp.float32)
    )
    hidden_grad = lax.psum_scatter(
        term.reshape(rows_dev, all_blocks * side).astype(jnp.bfloat16),
        "mp",
        scatter_dimension=1,
        tiled=True,
    ).astype(jnp.float32)
    pre_grad = (hidden_grad.reshape(rows_dev, local_cols, side) * silu_slope(pre)).astype(
        jnp.bfloat16
    )
    first_part = jnp.einsum(
        "rckf,rcg->ckfg", picked1, pre_grad, preferred_element_type=jnp.float32
    ).astype(jnp.bfloat16)
    bias_part = jnp.sum(pre_grad.astype(jnp.float32), axis=0).reshape(local_cols * side)
    first_grad, second_grad = (
        lax.psum_scatter(
            first_part.reshape(local_cols, -1).astype(jnp.float32).astype(jnp.bfloat16),
            "dp",
            scatter_dimension=1,
            tiled=True,
        ).astype(jnp.float32),
        lax.psum_scatter(
            second_part.reshape(local_cols, -1).astype(jnp.float32).astype(jnp.bfloat16),
            "dp",
            scatter_dimension=1,
            tiled=True,
        ).astype(jnp.float32),
    )
    bias_grad = lax.psum(bias_part, "dp")
    return (second_out.reshape(rows_dev, local_cols * side), first_grad, second_grad, bias_grad)


def solution(mesh):
    return jax.shard_map(
        body,
        mesh=mesh,
        in_specs=(
            P("dp", None),
            P(None, "dp", None),
            P("dp", None),
            P("mp", None),
            P("mp", None, None, None),
            P("mp"),
            P("mp", None),
            P("mp", None, None, None),
            P("dp", "mp"),
        ),
        out_specs=(P("dp", "mp"), P("mp", "dp"), P("mp", "dp"), P("mp")),
        check_vma=False,
    )
```

profile of v0, /device:TPU:0, one launch (start us, length us, event | category | flops | bytes accessed | tf_op | source)
XLA Modules:
  0.0 676.6 jit_solution(4836541255533304525)
XLA Ops:
  10.2 7.8 %broadcast_in_dim.24 = f32[512,64,128]{2,0,1:T(8,128)} broadcast(f32[]{:T(128)} %constant.87.clone.1), dimensions={} | broadcast | bytes 16777220 | tf_op jit(solution)/shard_map/broadcast_in_dim | solution.py:76
  18.0 214.6 %while.13 = (s32[]{:T(128)}, f32[512,64,128]{2,0,1:T(8,128)}, s32[16,16]{1,0:T(8,128)S(1)}, bf16[512,16,128]{0,2,1:T(8,128)(2,1)S(1)}, bf16[16,16,128,128]{3,2,1,0:T(8,128)(2,1)}, /*index=5*/s32[]{:T(128)}) while((s32[]{:T(128)}, f32[512,64,128]{2,0,1:T(8,128)}, s32[16,16]{1,0:T(8,128)S(1)}, bf16[512,16,128]{0,2,1:T(8,128)(2,1)S(1)}, ...), condition=%wide.region_3.4_spmd, body=%wide.region_1.3_spmd.sunk | while | flops 269484096 | bytes 17433872 | solution.py:75
  18.0 3.7 convolution_bitcast_fusion.2
  21.7 9.8 %scatter_fusion = f32[512,64,128]{2,0,1:T(8,128)} fusion(f32[512,64,128]{2,0,1:T(8,128)} %get-tuple-element.172, s32[16]{0:T(128)S(1)} %fusion.37, f32[16,512,128]{2,1,0:T(8,128)} %convolution_bitcast_fusion.2), kind=kCustom, calls=%fused_computation.5.clone.1 | custom fusion | flops 1048576 | bytes 12582976 | tf_op jit(solution)/shard_map/while/body/eval_jaxpr/scatter-add | solution.py:73
  31.5 3.7 convolution_bitcast_fusion.2
  35.2 9.7 %scatter_fusion = f32[512,64,128]{2,0,1:T(8,128)} fusion(f32[512,64,128]{2,0,1:T(8,128)} %get-tuple-element.172, s32[16]{0:T(128)S(1)} %fusion.37, f32[16,512,128]{2,1,0:T(8,128)} %convolution_bitcast_fusion.2), kind=kCustom, calls=%fused_computation.5.clone.1 | custom fusion | flops 1048576 | bytes 12582976 | tf_op jit(solution)/shard_map/while/body/eval_jaxpr/scatter-add | solution.py:73
  48.6 9.7 %scatter_fusion = f32[512,64,128]{2,0,1:T(8,128)} fusion(f32[512,64,128]{2,0,1:T(8,128)} %get-tuple-element.172, s32[16]{0:T(128)S(1)} %fusion.37, f32[16,512,128]{2,1,0:T(8,128)} %convolution_bitcast_fusion.2), kind=kCustom, calls=%fused_computation.5.clone.1 | custom fusion | flops 1048576 | bytes 12582976 | tf_op jit(solution)/shard_map/while/body/eval_jaxpr/scatter-add | solution.py:73
  58.3 3.7 convolution_bitcast_fusion.2
  62.0 9.7 %scatter_fusion = f32[512,64,128]{2,0,1:T(8,128)} fusion(f32[512,64,128]{2,0,1:T(8,128)} %get-tuple-element.172, s32[16]{0:T(128)S(1)} %fusion.37, f32[16,512,128]{2,1,0:T(8,128)} %convolution_bitcast_fusion.2), kind=kCustom, calls=%fused_computation.5.clone.1 | custom fusion | flops 1048576 | bytes 12582976 | tf_op jit(solution)/shard_map/while/body/eval_jaxpr/scatter-add | solution.py:73
  71.7 3.7 convolution_bitcast_fusion.2
  75.4 9.6 %scatter_fusion = f32[512,64,128]{2,0,1:T(8,128)} fusion(f32[512,64,128]{2,0,1:T(8,128)} %get-tuple-element.172, s32[16]{0:T(128)S(1)} %fusion.37, f32[16,512,128]{2,1,0:T(8,128)} %convolution_bitcast_fusion.2), kind=kCustom, calls=%fused_computation.5.clone.1 | custom fusion | flops 1048576 | bytes 12582976 | tf_op jit(solution)/shard_map/while/body/eval_jaxpr/scatter-add | solution.py:73
  85.0 3.7 convolution_bitcast_fusion.2
  88.8 9.7 %scatter_fusion = f32[512,64,128]{2,0,1:T(8,128)} fusion(f32[512,64,128]{2,0,1:T(8,128)} %get-tuple-element.172, s32[16]{0:T(128)S(1)} %fusion.37, f32[16,512,128]{2,1,0:T(8,128)} %convolution_bitcast_fusion.2), kind=kCustom, calls=%fused_computation.5.clone.1 | custom fusion | flops 1048576 | bytes 12582976 | tf_op jit(solution)/shard_map/while/body/eval_jaxpr/scatter-add | solution.py:73
  98.5 3.7 convolution_bitcast_fusion.2
  102.2 9.6 %scatter_fusion = f32[512,64,128]{2,0,1:T(8,128)} fusion(f32[512,64,128]{2,0,1:T(8,128)} %get-tuple-element.172, s32[16]{0:T(128)S(1)} %fusion.37, f32[16,512,128]{2,1,0:T(8,128)} %convolution_bitcast_fusion.2), kind=kCustom, calls=%fused_computation.5.clone.1 | custom fusion | flops 1048576 | bytes 12582976 | tf_op jit(solution)/shard_map/while/body/eval_jaxpr/scatter-add | solution.py:73
  111.8 3.7 convolution_bitcast_fusion.2
  115.5 9.7 %scatter_fusion = f32[512,64,128]{2,0,1:T(8,128)} fusion(f32[512,64,128]{2,0,1:T(8,128)} %get-tuple-element.172, s32[16]{0:T(128)S(1)} %fusion.37, f32[16,512,128]{2,1,0:T(8,128)} %convolution_bitcast_fusion.2), kind=kCustom, calls=%fused_computation.5.clone.1 | custom fusion | flops 1048576 | bytes 12582976 | tf_op jit(solution)/shard_map/while/body/eval_jaxpr/scatter-add | solution.py:73
  125.2 3.7 convolution_bitcast_fusion.2
  128.9 9.7 %scatter_fusion = f32[512,64,128]{2,0,1:T(8,128)} fusion(f32[512,64,128]{2,0,1:T(8,128)} %get-tuple-element.172, s32[16]{0:T(128)S(1)} %fusion.37, f32[16,512,128]{2,1,0:T(8,128)} %convolution_bitcast_fusion.2), kind=kCustom, calls=%fused_computation.5.clone.1 | custom fusion | flops 1048576 | bytes 12582976 | tf_op jit(solution)/shard_map/while/body/eval_jaxpr/scatter-add | solution.py:73
  138.7 3.7 convolution_bitcast_fusion.2
  142.4 9.7 %scatter_fusion = f32[512,64,128]{2,0,1:T(8,128)} fusion(f32[512,64,128]{2,0,1:T(8,128)} %get-tuple-element.172, s32[16]{0:T(128)S(1)} %fusion.37, f32[16,512,128]{2,1,0:T(8,128)} %convolution_bitcast_fusion.2), kind=kCustom, calls=%fused_computation.5.clone.1 | custom fusion | flops 1048576 | bytes 12582976 | tf_op jit(solution)/shard_map/while/body/eval_jaxpr/scatter-add | solution.py:73
  152.1 3.7 convolution_bitcast_fusion.2
  155.8 9.6 %scatter_fusion = f32[512,64,128]{2,0,1:T(8,128)} fusion(f32[512,64,128]{2,0,1:T(8,128)} %get-tuple-element.172, s32[16]{0:T(128)S(1)} %fusion.37, f32[16,512,128]{2,1,0:T(8,128)} %convolution_bitcast_fusion.2), kind=kCustom, calls=%fused_computation.5.clone.1 | custom fusion | flops 1048576 | bytes 12582976 | tf_op jit(solution)/shard_map/while/body/eval_jaxpr/scatter-add | solution.py:73
  165.5 3.7 convolution_bitcast_fusion.2
  169.2 9.7 %scatter_fusion = f32[512,64,128]{2,0,1:T(8,128)} fusion(f32[512,64,128]{2,0,1:T(8,128)} %get-tuple-element.172, s32[16]{0:T(128)S(1)} %fusion.37, f32[16,512,128]{2,1,0:T(8,128)} %convolution_bitcast_fusion.2), kind=kCustom, calls=%fused_computation.5.clone.1 | custom fusion | flops 1048576 | bytes 12582976 | tf_op jit(solution)/shard_map/while/body/eval_jaxpr/scatter-add | solution.py:73
  178.8 3.7 convolution_bitcast_fusion.2
  182.5 9.7 %scatter_fusion = f32[512,64,128]{2,0,1:T(8,128)} fusion(f32[512,64,128]{2,0,1:T(8,128)} %get-tuple-element.172, s32[16]{0:T(128)S(1)} %fusion.37, f32[16,512,128]{2,1,0:T(8,128)} %convolution_bitcast_fusion.2), kind=kCustom, calls=%fused_computation.5.clone.1 | custom fusion | flops 1048576 | bytes 12582976 | tf_op jit(solution)/shard_map/while/body/eval_jaxpr/scatter-add | solution.py:73
  192.3 3.7 convolution_bitcast_fusion.2
  196.0 9.7 %scatter_fusion = f32[512,64,128]{2,0,1:T(8,128)} fusion(f32[512,64,128]{2,0,1:T(8,128)} %get-tuple-element.172, s32[16]{0:T(128)S(1)} %fusion.37, f32[16,512,128]{2,1,0:T(8,128)} %convolution_bitcast_fusion.2), kind=kCustom, calls=%fused_computation.5.clone.1 | custom fusion | flops 1048576 | bytes 12582976 | tf_op jit(solution)/shard_map/while/body/eval_jaxpr/scatter-add | solution.py:73
  205.7 3.7 convolution_bitcast_fusion.2
  209.4 9.7 %scatter_fusion = f32[512,64,128]{2,0,1:T(8,128)} fusion(f32[512,64,128]{2,0,1:T(8,128)} %get-tuple-element.172, s32[16]{0:T(128)S(1)} %fusion.37, f32[16,512,128]{2,1,0:T(8,128)} %convolution_bitcast_fusion.2), kind=kCustom, calls=%fused_computation.5.clone.1 | custom fusion | flops 1048576 | bytes 12582976 | tf_op jit(solution)/shard_map/while/body/eval_jaxpr/scatter-add | solution.py:73
  219.1 3.7 convolution_bitcast_fusion.2
  222.8 9.7 %scatter_fusion = f32[512,64,128]{2,0,1:T(8,128)} fusion(f32[512,64,128]{2,0,1:T(8,128)} %get-tuple-element.172, s32[16]{0:T(128)S(1)} %fusion.37, f32[16,512,128]{2,1,0:T(8,128)} %convolution_bitcast_fusion.2), kind=kCustom, calls=%fused_computation.5.clone.1 | custom fusion | flops 1048576 | bytes 12582976 | tf_op jit(solution)/shard_map/while/body/eval_jaxpr/scatter-add | solution.py:73
  232.5 14.6 %copy.43 = bf16[512,64,128]{0,2,1:T(8,128)(2,1)} copy(f32[512,64,128]{2,0,1:T(8,128)} %get-tuple-element.98) | data formatting | bytes 25165824 | tf_op jit(solution)/shard_map/while | solution.py:75
  247.9 5.4 gather_fusion.2
  253.2 5.2 all-to-all-start
  260.2 24.8 %all-to-all-done = bf16[8,1,128,1024]{3,2,1,0:T(8,128)(2,1)S(1)} async-done(((bf16[8,1,128,1024]{3,2,1,0:T(8,128)(2,1)}), bf16[8,1,128,1024]{3,2,1,0:T(8,128)(2,1)S(1)}, u32[]{:S(2)}, u32[]{:S(2)}) %all-to-all-start) | async-done | bytes 2097184 | tf_op jit(solution)/shard_map/all_to_all | solution.py:43
  291.2 103.8 %reduce-scatter.4.cloned.1.call-done = bf16[512,2048]{0,1:T(8,128)(2,1)} async-done(((bf16[512,8192]{0,1:T(8,128)(2,1)}), bf16[512,2048]{0,1:T(8,128)(2,1)}) %reduce-scatter.4.cloned.1.call-update) | async-done | bytes 2097168 | tf_op jit(solution)/shard_map/reduce_scatter | solution.py:78
  395.0 7.3 %convert_reduce_fusion = (f32[16,128]{1,0:T(8,128)S(1)}, bf16[512,16,128]{0,2,1:T(8,128)(2,1)}, bf16[512,16,128]{0,2,1:T(8,128)(2,1)}) fusion(f32[16,128]{1,0:T(8,128)S(1)} %bitcast.146, bf16[512,16,128]{0,2,1:T(8,128)(2,1)} %bitcast.145, bf16[512,16,2,128]{3,0,2,1:T(8,128)(2,1)} %bitcast.131, bf16[16,2,128,128]{3,2,1,0:T(8,128)(2,1)S(1)} %copy-done), kind=kOutput, calls=%fused_computation.34 | convolution fusion | flops 552597504 | bytes 11550720 | tf_op jit(solution)/shard_map/rckf,ckfg->rcg/dot_general | solution.py:51
  402.7 6.5 copy.36
  409.2 4.0 fusion.17
  414.9 137.8 %all-gather.2.cloned.1.call-done = bf16[512,8192]{0,1:T(8,128)(2,1)} async-done(((bf16[512,2048]{0,1:T(8,128)(2,1)}), bf16[512,8192]{0,1:T(8,128)(2,1)}) %all-gather.2.cloned.1.call-update) | async-done | bytes 8388624 | tf_op jit(solution)/shard_map/all_gather | solution.py:55
  552.7 17.4 %gather_fusion.4 = bf16[256,512,128]{1,2,0:T(8,128)(2,1)} fusion(bf16[512,64,128]{0,2,1:T(8,128)(2,1)} %bitcast.126, s32[1024]{0:T(1024)S(1)} %pad_clamp_fusion), kind=kCustom, calls=%fused_computation.4 | custom fusion | bytes 67109888 | tf_op jit(solution)/shard_map/gather | solution.py:57
  570.1 17.3 %convolution_convert_fusion.1 = bf16[16,16,128,128]{3,2,1,0:T(8,128)(2,1)} fusion(bf16[512,16,16,128]{0,3,2,1:T(8,128)(2,1)} %bitcast.128, bf16[512,16,128,1]{0,2,3,1:T(8,128)(2,1)S(1)} %bitcast.139), kind=kOutput, calls=%fused_computation.18 | convolution fusion | flops 4299161600 | bytes 44040192 | tf_op jit(solution)/shard_map/rckf,rcg->ckfg/dot_general | solution.py:62
  587.3 10.3 %copy.67 = bf16[2,8,2048,128]{3,1,2,0:T(8,128)(2,1)} copy(bf16[2,8,2048,128]{3,2,1,0:T(8,128)(2,1)} %bitcast.133) | data formatting | bytes 16777216
  597.7 14.9 %psum.7 = f32[2048]{0:T(1024)} all-reduce(f32[2048]{0:T(1024)S(1)} %bitcast.144), channel_id=1, replica_groups=mesh['dp'=8,'mp'=4] {'dp'}, use_global_device_ids=true, to_apply=%region_8.9 | all-reduce | flops 2048 | bytes 16384 | tf_op jit(solution)/shard_map/psum | solution.py:105
  614.2 17.8 %bitcast_convert_fusion = bf16[16,512,128]{1,2,0:T(8,128)(2,1)S(1)} fusion(bf16[512,16,16,128]{0,3,2,1:T(8,128)(2,1)} %bitcast.129, bf16[16,16,128,128]{3,2,1,0:T(8,128)(2,1)} %get-tuple-element.201), kind=kOutput, calls=%fused_computation.21 | convolution fusion | flops 4296015872 | bytes 44040192 | tf_op jit(solution)/shard_map/rckf,ckfg->rcg/dot_general | solution.py:58
  634.4 33.0 %reduce-scatter.8.cloned.1.call-done = bf16[16,32768]{1,0:T(8,128)(2,1)} async-done(((bf16[16,262144]{1,0:T(8,128)(2,1)}), bf16[16,32768]{1,0:T(8,128)(2,1)}) %reduce-scatter.8.cloned.1.call-update) | async-done | bytes 1048592 | tf_op jit(solution)/shard_map/reduce_scatter | solution.py:98
  (72 shorter events, 24.1 us)
Async XLA Ops:
  7.2 387.8 %copy-start = (bf16[16,2,128,128]{3,2,1,0:T(8,128)(2,1)S(1)}, bf16[16,2,128,128]{3,2,1,0:T(8,128)(2,1)}, u32[]{:S(2)}) copy-start(bf16[16,2,128,128]{3,2,1,0:T(8,128)(2,1)} %param.15) | copy-start | bytes 3145732
  7.2 387.8 %reduce-scatter.4.cloned.1.call-start = ((), (), s32[]{:S(2)}) async-start(), calls=%async_computation.5 | async-start | bytes 10485760 | tf_op jit(solution)/shard_map/reduce_scatter | solution.py:78
  10.2 7.8 %copy-start.5 = (s32[16,16]{1,0:T(8,128)S(1)}, s32[16,16]{1,0:T(8,128)}, u32[]{:S(2)}) copy-start(s32[16,16]{1,0:T(8,128)} %param.17) | copy-start | bytes 3076
  232.5 14.6 %copy-start.3 = (bf16[512,16,128]{0,2,1:T(8,128)(2,1)}, bf16[512,16,128]{0,2,1:T(8,128)(2,1)S(1)}, u32[]{:S(2)}) copy-start(bf16[512,16,128]{0,2,1:T(8,128)(2,1)S(1)} %get-tuple-element.197) | copy-start | bytes 6291460
  247.2 0.7 copy-start.8
  247.8 10.7 %copy-start.2 = (s32[1,8]{1,0:T(1,128)S(1)}, s32[1,8]{1,0:T(1,128)}, u32[]{:S(2)}) copy-start(s32[1,8]{1,0:T(1,128)} %param.13) | copy-start | bytes 100
  247.8 12.2 %copy-start.6 = (s32[16,2]{0,1:T(2,128)S(1)}, s32[16,2]{0,1:T(2,128)}, u32[]{:S(2)}) copy-start(s32[16,2]{0,1:T(2,128)} %param.14) | copy-start | bytes 388
  253.2 31.8 %all-to-all-start = ((bf16[8,1,128,1024]{3,2,1,0:T(8,128)(2,1)}), bf16[8,1,128,1024]{3,2,1,0:T(8,128)(2,1)S(1)}, u32[]{:S(2)}, u32[]{:S(2)}) async-start(bf16[8,1,128,1024]{3,2,1,0:T(8,128)(2,1)} %bitcast.135), calls=%async_computation | async-start | bytes 4194304 | tf_op jit(solution)/shard_map/all_to_all | solution.py:43
  258.4 294.3 %all-gather.2.cloned.1.call-start = ((), (), s32[]{:S(2)}) async-start(), calls=%async_computation.4 | async-start | bytes 10485760 | tf_op jit(solution)/shard_map/all_gather | solution.py:55
  288.1 106.8 %copy-start.7 = (f32[2048]{0:T(1024)S(1)}, f32[2048]{0:T(1024)}, u32[]{:S(2)}) copy-start(f32[2048]{0:T(1024)} %param.16) | copy-start | bytes 24580
  402.3 210.3 %reduce-scatter.6.cloned.1.call-start = ((), (), s32[]{:S(2)}) async-start(), calls=%async_computation.6 | async-start | bytes 1179648 | tf_op jit(solution)/shard_map/reduce_scatter | solution.py:92
  402.7 6.6 copy-start.9
  414.9 252.5 %reduce-scatter.8.cloned.1.call-start = ((), (), s32[]{:S(2)}) async-start(), calls=%async_computation.7 | async-start | bytes 9437184 | tf_op jit(solution)/shard_map/reduce_scatter | solution.py:98
  552.7 17.4 %copy-start.4 = (bf16[512,16,128]{0,2,1:T(8,128)(2,1)S(1)}, bf16[512,16,128]{0,2,1:T(8,128)(2,1)}, u32[]{:S(2)}) copy-start(bf16[512,16,128]{0,2,1:T(8,128)(2,1)} %copy-done.3) | copy-start | bytes 6291460
  614.2 55.9 %copy-start.1 = (bf16[16,2,128,128]{3,2,1,0:T(8,128)(2,1)S(1)}, bf16[16,2,128,128]{3,2,1,0:T(8,128)(2,1)}, u32[]{:S(2)}) copy-start(bf16[16,2,128,128]{3,2,1,0:T(8,128)(2,1)} %param.15) | copy-start | bytes 3145732
Sparse Core Ops, SparseCore 0:
  247.3 147.5 reduce-scatter.3
  402.5 150.2 all-gather.1
  556.5 34.1 reduce-scatter.5
  597.8 69.5 reduce-scatter.7
where the time goes:
time: 679 us; the launch traced here: 677 us
  waiting for transfers between devices  299 us (44%)
  other arithmetic  160 us (24%)
  matrix products  106 us (16%)
  local copies, waits for them, and re-layouts  76.6 us (11%)
  blocking collectives  14.9 us (2%)
  between operations  13.9 us (2%)
    scatter-add x16, other arithmetic, add_column(): return total.at[:, where].add(spread)  155 us
    all_gather x1, waiting for transfers between devices, body(): whole_hidden = lax.all_gather(hidden, 'mp', axis=1, tiled=True)  138 us
    reduce_scatter x1, waiting for transfers between devices, body(): lax.psum_scatter(term.reshape(rows_dev, all_blocks * side).astype(jnp.bfl...  104 us
    dot_general x16, matrix products, add_column(): jnp.einsum('rg,kfg->rkf', up_column, weight_column, preferred_element_typ...  59.3 us
    reduce_scatter x1, waiting for transfers between devices, body(): lax.psum_scatter(second_part.reshape(local_cols, -1).astype(jnp.float32)....  33 us
    all_to_all x1, waiting for transfers between devices, body(): lax.all_to_all(sending, 'dp', split_axis=0, concat_axis=0, tiled=True)  24.8 us
    unnamed x25, local copies, waits for them, and re-layouts  19.1 us
    dot_general x1, matrix products, body(): jnp.einsum('rckf,ckfg->rcg', picked2, second_weight, preferred_element_ty...  17.8 us
  transfers between devices with their start and end apart: 5, of which 4 were waited for; matrix products, arithmetic and copies ran while one was open for 14% of the time, Pallas kernels for 0%

commit v1 on v0

v1 whole, which is shorter than its diff:
```python
import functools

import jax
import jax.numpy as jnp
from jax import lax
from jax.experimental import pallas as pl
from jax.experimental.pallas import tpu as pltpu
from jax.sharding import PartitionSpec as P

BF16 = jnp.bfloat16
F32 = jnp.float32


def params(mib):
    return pltpu.CompilerParams(vmem_limit_bytes=mib * 2**20)


def cost(flops, moved, trans=0):
    return pl.CostEstimate(flops=flops, bytes_accessed=moved, transcendentals=trans)


def dot(a, b):
    return jnp.dot(a, b, preferred_element_type=F32)


def pick_kernel(picks, stored, out):
    out[...] = stored[...]


def pick_blocks(picks, stored):
    slots, (_, side, width) = picks.shape[0], stored.shape
    return pl.pallas_call(
        pick_kernel,
        out_shape=jax.ShapeDtypeStruct((slots, side, width), stored.dtype),
        grid_spec=pltpu.PrefetchScalarGridSpec(
            num_scalar_prefetch=1,
            grid=(slots,),
            in_specs=[pl.BlockSpec((1, side, width), lambda i, p: (p[i], 0, 0))],
            out_specs=pl.BlockSpec((1, side, width), lambda i, p: (i, 0, 0)),
        ),
        name="pick",
    )(picks, stored)


def term_kernel(pattern, up, weight, out, acc):
    c = pl.program_id(0)
    keep, side = weight.shape[1], weight.shape[2]

    @pl.when(c == 0)
    def _():
        @pl.loop(0, acc.shape[0])
        def _(b):
            acc[b] = jnp.zeros(acc.shape[1:], F32)

    u = up[...]
    for k in range(0, keep, 2):
        pair = weight[0, k : k + 2].reshape(2 * side, side)
        spread = lax.dot_general(
            u, pair, (((1,), (1,)), ((), ())), preferred_element_type=F32
        )
        acc[pattern[c * keep + k]] += spread[:, :side]
        acc[pattern[c * keep + k + 1]] += spread[:, side:]

    @pl.when(c == pl.num_programs(0) - 1)
    def _():
        @pl.loop(0, acc.shape[0])
        def _(b):
            out[b] = acc[b].astype(BF16)


def hidden_term(pattern, cotangent, weight, all_blocks):
    cols, keep, side, _ = weight.shape
    rows = cotangent.shape[0]
    return pl.pallas_call(
        term_kernel,
        out_shape=jax.ShapeDtypeStruct((all_blocks, rows, side), BF16),
        grid_spec=pltpu.PrefetchScalarGridSpec(
            num_scalar_prefetch=1,
            grid=(cols,),
            in_specs=[
                pl.BlockSpec((rows, side), lambda c, p: (0, c)),
                pl.BlockSpec((1, keep, side, side), lambda c, p: (c, 0, 0, 0)),
            ],
            out_specs=pl.BlockSpec(
                (all_blocks, rows, side), lambda c, p: (0, 0, 0), pipeline_mode=pl.Buffered(1)
            ),
            scratch_shapes=[pltpu.VMEM((all_blocks, rows, side), F32)],
        ),
        compiler_params=params(40),
        cost_estimate=cost(2 * rows * cols * keep * side * side, 18 * 2**20),
        name="term",
    )(pattern.reshape(-1), cotangent, weight)


def first_kernel(
    pattern, source, got, weight, bias, part, hidden, hidden_t, grad, bias_part, x, xt
):
    step = pl.program_id(0)
    here, side = bias.shape[0], bias.shape[2]
    keep = weight.shape[0] * weight.shape[2] // (here * side)
    rows = x.shape[1]
    whole = weight[...].reshape(here, keep * side, side)

    @pl.when(step == 0)
    def _():
        for f in range(x.shape[0]):
            for j in range(rows // side):
                block = got[source[j], :, f * side : (f + 1) * side]
                x[f, j * side : (j + 1) * side, :] = block
                xt[f, :, j * side : (j + 1) * side] = block.T

    for i in range(here):
        at = [pattern[(step * here + i) * keep + k] for k in range(keep)]
        lhs = jnp.concatenate([x[a] for a in at], axis=1)
        v = dot(lhs, whole[i]) + bias[i]
        s = 1.0 / (1.0 + jnp.exp(-v))
        h = (v * s).astype(BF16)
        hidden[i] = h
        hidden_t[i] = h.T
        g = part[i].astype(F32) * (s * (1.0 + v * (1.0 - s)))
        bias_part[i] = jnp.sum(g, axis=0, keepdims=True)
        lhs_t = jnp.concatenate([xt[a] for a in at], axis=0)
        fg = dot(lhs_t, g.astype(BF16)).astype(BF16)
        grad[:, 0, i] = fg.reshape(grad.shape[0], -1, side)


def first_layer(pattern, source, got, weight, bias, part, n_mp, n_dp):
    blocks, keep = pattern.shape
    slots, side, width = got.shape
    rows = part.shape[1]
    local = blocks // n_mp
    here = 4 if local % 4 == 0 else 1
    per = local // here
    piece = keep * side // n_dp
    share = weight.shape[2]
    return pl.pallas_call(
        first_kernel,
        out_shape=(
            jax.ShapeDtypeStruct((blocks, rows, side), BF16),
            jax.ShapeDtypeStruct((blocks, side, rows), BF16),
            jax.ShapeDtypeStruct((n_dp, n_mp, local, piece, side), BF16),
            jax.ShapeDtypeStruct((blocks, 1, side), F32),
        ),
        grid_spec=pltpu.PrefetchScalarGridSpec(
            num_scalar_prefetch=2,
            grid=(blocks // here,),
            in_specs=[
                pl.BlockSpec(
                    (slots, side, width), lambda c, p, s: (0, 0, 0), pipeline_mode=pl.Buffered(1)
                ),
                pl.BlockSpec(
                    (n_dp // per, 1, share, side), lambda c, p, s: (c % per, c // per, 0, 0)
                ),
                pl.BlockSpec((here, 1, side), lambda c, p, s: (c, 0, 0)),
                pl.BlockSpec((here, rows, side), lambda c, p, s: (c, 0, 0)),
            ],
            out_specs=[
                pl.BlockSpec((here, rows, side), lambda c, p, s: (c, 0, 0)),
                pl.BlockSpec((here, side, rows), lambda c, p, s: (c, 0, 0)),
                pl.BlockSpec(
                    (n_dp, 1, here, piece, side), lambda c, p, s: (0, c // per, c % per, 0, 0)
                ),
                pl.BlockSpec((here, 1, side), lambda c, p, s: (c, 0, 0)),
            ],
            scratch_shapes=[
                pltpu.VMEM((width // side, rows, side), BF16),
                pltpu.VMEM((width // side, side, rows), BF16),
            ],
        ),
        compiler_params=params(32),
        cost_estimate=cost(4 * rows * blocks * keep * side * side, 30 * 2**20, 2**22),
        name="first",
    )(pattern.reshape(-1), source, got, weight, bias.reshape(blocks, 1, side), part)


def grad_kernel(pattern, hidden_t, up, out):
    c = pl.program_id(0)
    n, _, piece, side = out.shape
    keep = n * piece // side
    lhs = jnp.concatenate([hidden_t[pattern[c * keep + k]] for k in range(keep)], axis=0)
    out[:, 0] = dot(lhs, up[...]).astype(BF16).reshape(n, piece, side)


def second_gradient(pattern, hidden_t, cotangent, n_dp):
    cols, keep = pattern.shape
    blocks, side, rows = hidden_t.shape
    piece = keep * side // n_dp
    return pl.pallas_call(
        grad_kernel,
        out_shape=jax.ShapeDtypeStruct((n_dp, cols, piece, side), BF16),
        grid_spec=pltpu.PrefetchScalarGridSpec(
            num_scalar_prefetch=1,
            grid=(cols,),
            in_specs=[
                pl.BlockSpec(
                    (blocks, side, rows), lambda c, p: (0, 0, 0), pipeline_mode=pl.Buffered(1)
                ),
                pl.BlockSpec((rows, side), lambda c, p: (0, c)),
            ],
            out_specs=pl.BlockSpec((n_dp, 1, piece, side), lambda c, p: (0, c, 0, 0)),
        ),
        compiler_params=params(32),
        cost_estimate=cost(2 * rows * cols * keep * side * side, 18 * 2**20),
        name="second_grad",
    )(pattern.reshape(-1), hidden_t, cotangent)


def out_kernel(pattern, hidden, weight, out):
    c = pl.program_id(0)
    keep, side = weight.shape[1], weight.shape[2]
    lhs = jnp.concatenate([hidden[pattern[c * keep + k]] for k in range(keep)], axis=1)
    out[...] = dot(lhs, weight[0].reshape(keep * side, side)).astype(BF16)


def second_layer(pattern, hidden, weight):
    cols, keep, side, _ = weight.shape
    blocks, rows, _ = hidden.shape
    return pl.pallas_call(
        out_kernel,
        out_shape=jax.ShapeDtypeStruct((rows, cols * side), BF16),
        grid_spec=pltpu.PrefetchScalarGridSpec(
            num_scalar_prefetch=1,
            grid=(cols,),
            in_specs=[
                pl.BlockSpec(
                    (blocks, rows, side), lambda c, p: (0, 0, 0), pipeline_mode=pl.Buffered(1)
                ),
                pl.BlockSpec((1, keep, side, side), lambda c, p: (c, 0, 0, 0)),
            ],
            out_specs=pl.BlockSpec((rows, side), lambda c, p: (0, c)),
        ),
        compiler_params=params(32),
        cost_estimate=cost(2 * rows * cols * keep * side * side, 18 * 2**20),
        name="second_out",
    )(pattern.reshape(-1), hidden, weight)


def body(
    reservoir,
    pull_list,
    pull_counts,
    first_pattern,
    first_weight,
    first_bias,
    second_pattern,
    second_weight,
    cotangent,
):
    n_dp, n_mp = lax.axis_size("dp"), lax.axis_size("mp")
    d = lax.axis_index("dp")
    local, keep1, side, _ = first_weight.shape
    keep2 = second_weight.shape[1]
    width_in = reservoir.shape[1]
    cap = pull_list.shape[2]
    rows = cotangent.shape[0]
    slots = n_dp * cap
    blocks = local * n_mp

    stored = reservoir.reshape(-1, side, width_in)
    sending = pick_blocks(pull_list[:, 0, :].reshape(slots), stored)
    got = lax.all_to_all(sending, "dp", split_axis=0, concat_axis=0, tiled=True)

    flat = first_weight.reshape(-1, side)
    share = flat.shape[0] // n_dp
    mine = lax.dynamic_slice_in_dim(flat, d * share, share, 0)
    weight = lax.all_gather(mine, "mp", axis=0, tiled=True)
    weight = lax.all_gather(weight, "dp", axis=0, tiled=True)
    weight = weight.reshape(n_dp, n_mp, share, side)
    small = jnp.concatenate([first_bias, first_pattern.astype(F32).reshape(-1)])
    small = lax.all_gather(small, "mp", axis=0)
    bias = small[:, : local * side].reshape(blocks, side)
    pattern1 = small[:, local * side :].astype(jnp.int32).reshape(blocks, keep1)

    counts = pull_counts[0]
    position = jnp.arange(slots, dtype=jnp.int32)
    owner, within = position // cap, position % cap
    prefix = jnp.cumsum(counts) - counts
    dest = jnp.where(within < counts[owner], prefix[owner] + within, -1)
    match = dest[None, :] == jnp.arange(rows // side, dtype=jnp.int32)[:, None]
    source = jnp.sum(jnp.where(match, position[None, :], 0), axis=1).astype(jnp.int32)

    part = hidden_term(second_pattern, cotangent, second_weight, blocks)
    hidden, hidden_t, grad1, bias_part = first_layer(
        pattern1, source, got, weight, bias, part, n_mp, n_dp
    )
    grad1 = lax.psum_scatter(
        grad1.reshape(n_dp, -1, side), "dp", scatter_dimension=0, tiled=True
    )
    grad1 = lax.psum_scatter(
        grad1.reshape(n_mp, -1, side), "mp", scatter_dimension=0, tiled=True
    )
    grad2 = second_gradient(second_pattern, hidden_t, cotangent, n_dp)
    grad2 = lax.psum_scatter(
        grad2.reshape(n_dp, -1, side), "dp", scatter_dimension=0, tiled=True
    )
    second_out = second_layer(second_pattern, hidden, second_weight)
    bias_all = lax.psum(bias_part.reshape(n_mp, local * side), ("mp", "dp"))
    bias_grad = lax.dynamic_index_in_dim(bias_all, lax.axis_index("mp"), 0, keepdims=False)
    return (
        second_out,
        grad1.reshape(local, -1).astype(F32),
        grad2.reshape(local, -1).astype(F32),
        bias_grad,
    )


def solution(mesh):
    return jax.shard_map(
        body,
        mesh=mesh,
        in_specs=(
            P("dp", None),
            P(None, "dp", None),
            P("dp", None),
            P("mp", None),
            P("mp", None, None, None),
            P("mp"),
            P("mp", None),
            P("mp", None, None, None),
            P("dp", "mp"),
        ),
        out_specs=(P("dp", "mp"), P("mp", "dp"), P("mp", "dp"), P("mp")),
        check_vma=False,
    )
```

time: 679 us -> 273 us (0.40)
  waiting for transfers between devices: 299 us -> 64.7 us
  other arithmetic: 160 us -> 1.19 us
  matrix products: 106 us -> 0 us
  Pallas kernels: 0 us -> 75.1 us
  blocking collectives: 14.9 us -> 78.3 us
  local copies, waits for them, and re-layouts: 76.6 us -> 33.4 us
    scatter-add x16 -> x0, other arithmetic: 155 us -> none  [add_column(): return total.at[:, where].add(spread)]
    all_gather x1, waiting for transfers between devices: 138 us -> 0.01 us  [body(): weight = lax.all_gather(weight, 'dp', axis=0, tiled=True)]
    dot_general x21 -> x0, matrix products: 106 us -> none  [the longest x16 59.3 us: add_column(): jnp.einsum('rg,kfg->rkf', up_column, weight_column, preferred_element_typ...]
    pallas_call x0 -> x5, Pallas kernels: none -> 75.1 us  [the longest x1 23.5 us: first_layer(): pl.pallas_call(first_kernel, out_shape=(jax.ShapeDtypeStruct((blocks, row...]
    reduce_scatter x3, waiting for transfers between devices: 137 us -> 64.6 us  [the longest x1 49.9 us: body(): lax.psum_scatter(grad1.reshape(n_dp, -1, side), 'dp', scatter_dimension=0...]
    gather x4 -> x0, local copies, waits for them, and re-layouts: 32.4 us -> none  [the longest x1 17.4 us: body(): whole_hidden.reshape(rows_dev, all_blocks, side)[:, second_pattern]]
    psum x1, blocking collectives: 14.9 us -> 40 us  [body(): bias_all = lax.psum(bias_part.reshape(n_mp, local * side), ('mp', 'dp'))]
    all_to_all x1, waiting for transfers between devices: 24.8 us -> 0.01 us  [body(): got = lax.all_to_all(sending, 'dp', split_axis=0, concat_axis=0, tiled=True)]
  transfers between devices with their start and end apart: 5 -> 5, of which waited for: 4 -> 2; matrix products, arithmetic and copies ran while one was open for 14% -> 2% of each run, Pallas kernels for 0% -> 19%
where the time goes in v1:
time: 273 us; the launch traced here: 272 us
  blocking collectives  78.3 us (29%)
  Pallas kernels  75.1 us (28%)
  waiting for transfers between devices  64.7 us (24%)
  local copies, waits for them, and re-layouts  33.4 us (12%)
  between operations  14.6 us (5%)
  starting transfers between devices  4.67 us (2%)
    reduce_scatter x1, waiting for transfers between devices, body(): lax.psum_scatter(grad1.reshape(n_dp, -1, side), 'dp', scatter_dimension=0...  49.9 us
    psum x1, blocking collectives, body(): bias_all = lax.psum(bias_part.reshape(n_mp, local * side), ('mp', 'dp'))  40 us
    unnamed x34, local copies, waits for them, and re-layouts  26.3 us
    pallas_call x1, Pallas kernels, first_layer(): pl.pallas_call(first_kernel, out_shape=(jax.ShapeDtypeStruct((blocks, row...  23.5 us
    unnamed x1, blocking collectives  20.3 us
    pallas_call x1, Pallas kernels, hidden_term(): pl.pallas_call(term_kernel, out_shape=jax.ShapeDtypeStruct((all_blocks, r...  19.6 us
    all_gather x1, blocking collectives, body(): weight = lax.all_gather(mine, 'mp', axis=0, tiled=True)  18 us
    reduce_scatter x1, waiting for transfers between devices, body(): lax.psum_scatter(grad2.reshape(n_dp, -1, side), 'dp', scatter_dimension=0...  14.7 us
  transfers between devices with their start and end apart: 5, of which 2 were waited for; matrix products, arithmetic and copies ran while one was open for 2% of the time, Pallas kernels for 19%

profile of v1, /device:TPU:0, one launch (start us, length us, event | category | flops | bytes accessed | tf_op | source)
XLA Modules:
  0.0 271.9 jit_solution(5911194459497424038)
XLA Ops:
  7.2 0.0 copy-start
  7.2 0.0 all-gather.3.cloned.1.call-start
  7.2 1.2 copy-done
  8.4 18.0 %all_gather.14 = bf16[2048,128]{1,0:T(8,128)(2,1)} all-gather(bf16[512,128]{1,0:T(8,128)(2,1)S(1)} %constant_dynamic-slice_fusion), channel_id=1, replica_groups=mesh['dp'=8,'mp'=4] {'mp'}, dimensions={0}, use_global_device_ids=true | all-gather | bytes 655360 | tf_op jit(solution)/shard_map/all_gather | solution.py:266
  26.4 0.0 all-gather.3.cloned.1.call-update
  26.4 6.3 %pick.1 = bf16[8,128,1024]{2,1,0:T(8,128)(2,1)} custom-call(s32[8]{0:T(128)} %bitcast.23, bf16[32,128,1024]{2,1,0:T(8,128)(2,1)} %bitcast.20), custom_call_target="tpu_custom_call" | custom-call | tf_op jit(solution)/shard_map/pick/pallas_call | solution.py:32
  32.8 0.0 copy-start.11
  32.8 0.0 copy-start.4
  32.8 4.5 %all-to-all-start = ((bf16[8,128,1024]{2,1,0:T(8,128)(2,1)}), bf16[8,128,1024]{2,1,0:T(8,128)(2,1)}, u32[]{:S(2)}, u32[]{:S(2)}) async-start(bf16[8,128,1024]{2,1,0:T(8,128)(2,1)} %pick.1), calls=%async_computation | async-start | bytes 4194304 | tf_op jit(solution)/shard_map/all_to_all | solution.py:261
  37.3 0.0 reduce-scatter.4.cloned.1.call-start
  37.4 0.1 copy.15
  37.5 0.1 reshape.78
  37.6 0.6 dynamic-slice
  38.8 0.1 maximum_dynamic-update-slice_fusion
  39.0 20.3 %all-reduce = f32[8320]{0:T(1024)S(1)} all-reduce(f32[8320]{0:T(1024)S(1)} %maximum_dynamic-update-slice_fusion), channel_id=2, replica_groups=mesh['dp'=8,'mp'=4] {'mp'}, use_global_device_ids=true, to_apply=%add | all-reduce | flops 8320 | bytes 66560
  59.3 0.1 reshape.106
  59.4 0.1 reshape_reshape.7.bias
  59.5 0.1 reshape_reshape.6.pattern
  59.6 0.1 reshape.77.pattern
  59.6 0.2 reduce-window.9
  59.8 0.6 gather_fusion.1
  60.5 0.6 gather_fusion
  61.1 0.1 select_reduce_fusion.source
  61.3 19.6 %term.1.part = bf16[64,512,128]{2,1,0:T(8,128)(2,1)S(1)} custom-call(s32[256]{0:T(256)S(1)} %reshape.77.pattern, bf16[512,2048]{1,0:T(8,128)(2,1)S(1)} %copy-done.4, bf16[16,16,128,128]{3,2,1,0:T(8,128)(2,1)} %weight.3), custom_call_target="tpu_custom_call" | custom-call | flops 4294967296 | bytes 18874368 | tf_op jit(solution)/shard_map/term/pallas_call | solution.py:74
  80.9 3.2 %copy-done.8 = bf16[64,512,128]{2,1,0:T(8,128)(2,1)} copy-done((bf16[64,512,128]{2,1,0:T(8,128)(2,1)}, bf16[64,512,128]{2,1,0:T(8,128)(2,1)S(1)}, u32[]{:S(2)}) %copy-start.8) | copy-done | bytes 8388632
  84.2 2.2 copy-done.10
  86.3 23.5 %first.1 = (bf16[64,512,128]{2,1,0:T(8,128)(2,1)S(1)}, bf16[64,128,512]{2,1,0:T(8,128)(2,1)}, bf16[8,4,16,32,128]{4,3,2,1,0:T(8,128)(2,1)S(1)}, f32[64,1,128]{2,1,0:T(1,128)S(1)}) custom-call(s32[128]{0:T(128)S(1)} %reshape_reshape.6.pattern, s32[4]{0:T(128)S(1)} %select_reduce_fusion.source, bf16[8,128,1024]{2,1,0:T(8,128)(2,1)} %all-to-all-done.got, ...), custom_call_target="tpu_custom_call" | custom-call | flops 4294967296 | bytes 31457280 | tf_op jit(solution)/shard_map/first/pallas_call | solution.py:136
  109.8 3.2 %copy-done.5 = bf16[64,512,128]{2,1,0:T(8,128)(2,1)} copy-done((bf16[64,512,128]{2,1,0:T(8,128)(2,1)}, bf16[64,512,128]{2,1,0:T(8,128)(2,1)S(1)}, u32[]{:S(2)}) %copy-start.5) | copy-done | bytes 8388632
  113.1 1.9 copy-done.9
  115.0 0.0 reduce-scatter.4.cloned.1.call-update
  115.0 0.0 reduce-scatter.6.cloned.1.call-start
  115.1 49.9 %reduce-scatter.4.cloned.1.call-done = bf16[1,2048,128]{2,1,0:T(8,128)(2,1)} async-done(((bf16[8,2048,128]{2,1,0:T(8,128)(2,1)}), bf16[1,2048,128]{2,1,0:T(8,128)(2,1)}) %reduce-scatter.4.cloned.1.call-update) | async-done | bytes 524304 | tf_op jit(solution)/shard_map/reduce_scatter | solution.py:286
  165.0 0.0 reduce-scatter.6.cloned.1.call-update
  165.0 0.0 reduce-scatter.8.cloned.1.call-start
  165.1 3.4 %copy-done.7 = bf16[64,128,512]{2,1,0:T(8,128)(2,1)S(1)} copy-done((bf16[64,128,512]{2,1,0:T(8,128)(2,1)S(1)}, bf16[64,128,512]{2,1,0:T(8,128)(2,1)}, u32[]{:S(2)}) %copy-start.7) | copy-done | bytes 8388632
  168.4 12.8 %second_grad.1 = bf16[8,16,256,128]{3,2,1,0:T(8,128)(2,1)S(1)} custom-call(s32[256]{0:T(256)S(1)} %reshape.77.pattern, bf16[64,128,512]{2,1,0:T(8,128)(2,1)S(1)} %copy-done.7, bf16[512,2048]{1,0:T(8,128)(2,1)S(1)} %copy-done.4), custom_call_target="tpu_custom_call" | custom-call | flops 4294967296 | bytes 18874368 | tf_op jit(solution)/shard_map/second_grad/pallas_call | solution.py:188
  181.3 3.2 %copy-done.3 = bf16[8,16,256,128]{3,2,1,0:T(8,128)(2,1)} copy-done((bf16[8,16,256,128]{3,2,1,0:T(8,128)(2,1)}, bf16[8,16,256,128]{3,2,1,0:T(8,128)(2,1)S(1)}, u32[]{:S(2)}) %copy-start.3) | copy-done | bytes 8388632
  184.5 0.0 reduce-scatter.8.cloned.1.call-update
  184.6 0.5 broadcast.63
  185.1 0.7 reduce.3
  185.8 40.0 %psum.7 = f32[4,2048]{1,0:T(4,128)S(1)} all-reduce(f32[4,2048]{1,0:T(4,128)S(1)} %reshape.87), channel_id=1, replica_groups=mesh['dp'=8,'mp'=4] {'mp','dp'}, use_global_device_ids=true, to_apply=%region_5.6 | all-reduce | flops 8192 | bytes 65536 | tf_op jit(solution)/shard_map/psum | solution.py:297
  225.8 0.6 constant_dynamic-slice_fusion.1
  226.4 3.6 %copy-done.2 = bf16[16,16,128,128]{3,2,1,0:T(8,128)(2,1)S(1)} copy-done((bf16[16,16,128,128]{3,2,1,0:T(8,128)(2,1)S(1)}, bf16[16,16,128,128]{3,2,1,0:T(8,128)(2,1)}, u32[]{:S(2)}) %copy-start.2) | copy-done | bytes 8388632
  230.0 3.6 %copy-done.6 = bf16[64,512,128]{2,1,0:T(8,128)(2,1)S(1)} copy-done((bf16[64,512,128]{2,1,0:T(8,128)(2,1)S(1)}, bf16[64,512,128]{2,1,0:T(8,128)(2,1)}, u32[]{:S(2)}) %copy-start.6) | copy-done | bytes 8388632
  233.7 12.8 %second_out.1 = bf16[512,2048]{1,0:T(8,128)(2,1)} custom-call(s32[256]{0:T(256)S(1)} %reshape.77.pattern, bf16[64,512,128]{2,1,0:T(8,128)(2,1)S(1)} %copy-done.6, bf16[16,16,128,128]{3,2,1,0:T(8,128)(2,1)S(1)} %copy-done.2), custom_call_target="tpu_custom_call" | custom-call | flops 4294967296 | bytes 18874368 | tf_op jit(solution)/shard_map/second_out/pallas_call | solution.py:218
  246.5 1.7 reshape.88
  248.1 14.7 %reduce-scatter.8.cloned.1.call-done = bf16[1,4096,128]{2,1,0:T(8,128)(2,1)} async-done(((bf16[8,4096,128]{2,1,0:T(8,128)(2,1)}), bf16[1,4096,128]{2,1,0:T(8,128)(2,1)}) %reduce-scatter.8.cloned.1.call-update) | async-done | bytes 1048592 | tf_op jit(solution)/shard_map/reduce_scatter | solution.py:293
  262.8 2.6 reshape.89
  (33 shorter events, 0.1 us)
Async XLA Ops:
  7.2 1.2 copy-start
  7.2 77.0 %all-gather.3.cloned.1.call-start = ((), (), s32[]{:S(2)}) async-start(), calls=%async_computation.4 | async-start | bytes 4718592 | tf_op jit(solution)/shard_map/all_gather | solution.py:267
  32.8 4.6 %copy-start.14 = (s32[16,2]{0,1:T(2,128)S(1)}, s32[16,2]{0,1:T(2,128)}, u32[]{:S(2)}) copy-start(s32[16,2]{0,1:T(2,128)} %param.12) | copy-start | bytes 388
  32.8 4.8 %copy-start.15 = (u32[32]{0:T(128)S(1)}, u32[32]{0:T(128)}, u32[]{:S(2)}) copy-start(u32[32]{0:T(128)} %constant.55) | copy-start | bytes 388
  32.8 6.1 %copy-start.13 = (f32[2048]{0:T(1024)S(1)}, f32[2048]{0:T(1024)}, u32[]{:S(2)}) copy-start(f32[2048]{0:T(1024)} %param.14) | copy-start | bytes 24580
  32.8 26.8 %copy-start.12 = (s32[16,16]{1,0:T(8,128)S(1)}, s32[16,16]{1,0:T(8,128)}, u32[]{:S(2)}) copy-start(s32[16,16]{1,0:T(8,128)} %param.15) | copy-start | bytes 3076
  32.8 26.9 %copy-start.11 = (s32[1,8]{1,0:T(1,128)S(1)}, s32[1,8]{1,0:T(1,128)}, u32[]{:S(2)}) copy-start(s32[1,8]{1,0:T(1,128)} %param.11) | copy-start | bytes 100
  32.8 28.5 %copy-start.4 = (bf16[512,2048]{1,0:T(8,128)(2,1)S(1)}, bf16[512,2048]{1,0:T(8,128)(2,1)}, u32[]{:S(2)}) copy-start(bf16[512,2048]{1,0:T(8,128)(2,1)} %up.3) | copy-start | bytes 6291460
  32.8 51.3 %all-to-all-start = ((bf16[8,128,1024]{2,1,0:T(8,128)(2,1)}), bf16[8,128,1024]{2,1,0:T(8,128)(2,1)}, u32[]{:S(2)}, u32[]{:S(2)}) async-start(bf16[8,128,1024]{2,1,0:T(8,128)(2,1)} %pick.1), calls=%async_computation | async-start | bytes 4194304 | tf_op jit(solution)/shard_map/all_to_all | solution.py:261
  37.3 127.7 %reduce-scatter.4.cloned.1.call-start = ((), (), s32[]{:S(2)}) async-start(), calls=%async_computation.5 | async-start | bytes 4718592 | tf_op jit(solution)/shard_map/reduce_scatter | solution.py:286
  80.9 3.2 %copy-start.8 = (bf16[64,512,128]{2,1,0:T(8,128)(2,1)}, bf16[64,512,128]{2,1,0:T(8,128)(2,1)S(1)}, u32[]{:S(2)}) copy-start(bf16[64,512,128]{2,1,0:T(8,128)(2,1)S(1)} %term.1.part) | copy-start | bytes 25165828
  84.2 2.2 copy-start.10
  109.8 3.2 %copy-start.5 = (bf16[64,512,128]{2,1,0:T(8,128)(2,1)}, bf16[64,512,128]{2,1,0:T(8,128)(2,1)S(1)}, u32[]{:S(2)}) copy-start(bf16[64,512,128]{2,1,0:T(8,128)(2,1)S(1)} %get-tuple-element.8.hidden) | copy-start | bytes 25165828
  113.1 1.9 copy-start.9
  115.0 131.5 %reduce-scatter.6.cloned.1.call-start = ((), (), s32[]{:S(2)}) async-start(), calls=%async_computation.6 | async-start | bytes 655360 | tf_op jit(solution)/shard_map/reduce_scatter | solution.py:289
  165.0 97.8 %reduce-scatter.8.cloned.1.call-start = ((), (), s32[]{:S(2)}) async-start(), calls=%async_computation.7 | async-start | bytes 9437184 | tf_op jit(solution)/shard_map/reduce_scatter | solution.py:293
  165.1 3.4 %copy-start.7 = (bf16[64,128,512]{2,1,0:T(8,128)(2,1)S(1)}, bf16[64,128,512]{2,1,0:T(8,128)(2,1)}, u32[]{:S(2)}) copy-start(bf16[64,128,512]{2,1,0:T(8,128)(2,1)} %get-tuple-element.10.hidden_t) | copy-start | bytes 25165828
  181.3 3.2 %copy-start.3 = (bf16[8,16,256,128]{3,2,1,0:T(8,128)(2,1)}, bf16[8,16,256,128]{3,2,1,0:T(8,128)(2,1)S(1)}, u32[]{:S(2)}) copy-start(bf16[8,16,256,128]{3,2,1,0:T(8,128)(2,1)S(1)} %second_grad.1) | copy-start | bytes 25165828
  226.4 3.7 %copy-start.2 = (bf16[16,16,128,128]{3,2,1,0:T(8,128)(2,1)S(1)}, bf16[16,16,128,128]{3,2,1,0:T(8,128)(2,1)}, u32[]{:S(2)}) copy-start(bf16[16,16,128,128]{3,2,1,0:T(8,128)(2,1)} %weight.3) | copy-start | bytes 25165828
  230.0 3.7 %copy-start.6 = (bf16[64,512,128]{2,1,0:T(8,128)(2,1)S(1)}, bf16[64,512,128]{2,1,0:T(8,128)(2,1)}, u32[]{:S(2)}) copy-start(bf16[64,512,128]{2,1,0:T(8,128)(2,1)} %copy-done.5) | copy-start | bytes 25165828
  233.7 31.7 %copy-start.1 = (bf16[16,2,128,128]{3,2,1,0:T(8,128)(2,1)S(1)}, bf16[16,2,128,128]{3,2,1,0:T(8,128)(2,1)}, u32[]{:S(2)}) copy-start(bf16[16,2,128,128]{3,2,1,0:T(8,128)(2,1)} %param.13) | copy-start | bytes 3145732
Sparse Core Ops, SparseCore 0:
  26.6 54.2 all-gather.2
  115.1 49.8 reduce-scatter.3
  167.3 21.8 reduce-scatter.5
  192.5 70.2 reduce-scatter.7

commit v2 on v1

--- a/solution.py
+++ b/solution.py
@@ -121,10 +121,11 @@
         bias_part[i] = jnp.sum(g, axis=0, keepdims=True)
         lhs_t = jnp.concatenate([xt[a] for a in at], axis=0)
         fg = dot(lhs_t, g.astype(BF16)).astype(BF16)
-        grad[:, 0, i] = fg.reshape(grad.shape[0], -1, side)
-
-
-def first_layer(pattern, source, got, weight, bias, part, n_mp, n_dp):
+        piece = keep * side // grad.shape[0]
+        grad[:, i * piece : (i + 1) * piece] = fg.reshape(-1, piece, side)
+
+
+def first_layer(pattern, source, got, weight, bias, part, n_mp, n_dp, extra):
     blocks, keep = pattern.shape
     slots, side, width = got.shape
     rows = part.shape[1]
@@ -138,7 +139,7 @@
         out_shape=(
             jax.ShapeDtypeStruct((blocks, rows, side), BF16),
             jax.ShapeDtypeStruct((blocks, side, rows), BF16),
-            jax.ShapeDtypeStruct((n_dp, n_mp, local, piece, side), BF16),
+            jax.ShapeDtypeStruct((n_dp, blocks * piece + extra, side), BF16),
             jax.ShapeDtypeStruct((blocks, 1, side), F32),
         ),
         grid_spec=pltpu.PrefetchScalarGridSpec(
@@ -157,9 +158,7 @@
             out_specs=[
                 pl.BlockSpec((here, rows, side), lambda c, p, s: (c, 0, 0)),
                 pl.BlockSpec((here, side, rows), lambda c, p, s: (c, 0, 0)),
-                pl.BlockSpec(
-                    (n_dp, 1, here, piece, side), lambda c, p, s: (0, c // per, c % per, 0, 0)
-                ),
+                pl.BlockSpec((n_dp, here * piece, side), lambda c, p, s: (0, c, 0)),
                 pl.BlockSpec((here, 1, side), lambda c, p, s: (c, 0, 0)),
             ],
             scratch_shapes=[
@@ -173,21 +172,23 @@
     )(pattern.reshape(-1), source, got, weight, bias.reshape(blocks, 1, side), part)
 
 
-def grad_kernel(pattern, hidden_t, up, out):
+def grad_kernel(pattern, hidden_t, up, both, out):
     c = pl.program_id(0)
-    n, _, piece, side = out.shape
+    n, piece, side = out.shape
     keep = n * piece // side
     lhs = jnp.concatenate([hidden_t[pattern[c * keep + k]] for k in range(keep)], axis=0)
-    out[:, 0] = dot(lhs, up[...]).astype(BF16).reshape(n, piece, side)
-
-
-def second_gradient(pattern, hidden_t, cotangent, n_dp):
+    out[...] = dot(lhs, up[...]).astype(BF16).reshape(n, piece, side)
+
+
+def second_gradient(pattern, hidden_t, cotangent, both):
     cols, keep = pattern.shape
     blocks, side, rows = hidden_t.shape
+    n_dp, total, _ = both.shape
     piece = keep * side // n_dp
+    skip = total // piece - cols
     return pl.pallas_call(
         grad_kernel,
-        out_shape=jax.ShapeDtypeStruct((n_dp, cols, piece, side), BF16),
+        out_shape=jax.ShapeDtypeStruct(both.shape, BF16),
         grid_spec=pltpu.PrefetchScalarGridSpec(
             num_scalar_prefetch=1,
             grid=(cols,),
@@ -196,13 +197,15 @@
                     (blocks, side, rows), lambda c, p: (0, 0, 0), pipeline_mode=pl.Buffered(1)
                 ),
                 pl.BlockSpec((rows, side), lambda c, p: (0, c)),
-            ],
-            out_specs=pl.BlockSpec((n_dp, 1, piece, side), lambda c, p: (0, c, 0, 0)),
-        ),
+                pl.BlockSpec(memory_space=pl.ANY),
+            ],
+            out_specs=pl.BlockSpec((n_dp, piece, side), lambda c, p: (0, skip + c, 0)),
+        ),
+        input_output_aliases={3: 0},
         compiler_params=params(32),
         cost_estimate=cost(2 * rows * cols * keep * side * side, 18 * 2**20),
         name="second_grad",
-    )(pattern.reshape(-1), hidden_t, cotangent)
+    )(pattern.reshape(-1), hidden_t, cotangent, both)
 
 
 def out_kernel(pattern, hidden, weight, out):
@@ -280,25 +283,24 @@
     source = jnp.sum(jnp.where(match, position[None, :], 0), axis=1).astype(jnp.int32)
 
     part = hidden_term(second_pattern, cotangent, second_weight, blocks)
-    hidden, hidden_t, grad1, bias_part = first_layer(
-        pattern1, source, got, weight, bias, part, n_mp, n_dp
+    extra = local * keep2 * side // n_dp
+    hidden, hidden_t, both, bias_part = first_layer(
+        pattern1, source, got, weight, bias, part, n_mp, n_dp, extra
     )
-    grad1 = lax.psum_scatter(
-        grad1.reshape(n_dp, -1, side), "dp", scatter_dimension=0, tiled=True
+    both = second_gradient(second_pattern, hidden_t, cotangent, both)
+    both = lax.psum_scatter(both, "dp", scatter_dimension=0, tiled=True)[0]
+    head = both.shape[0] - extra
+    grad1 = lax.all_to_all(
+        both[:head].reshape(n_mp, -1, side), "mp", split_axis=0, concat_axis=0, tiled=True
     )
-    grad1 = lax.psum_scatter(
-        grad1.reshape(n_mp, -1, side), "mp", scatter_dimension=0, tiled=True
-    )
-    grad2 = second_gradient(second_pattern, hidden_t, cotangent, n_dp)
-    grad2 = lax.psum_scatter(
-        grad2.reshape(n_dp, -1, side), "dp", scatter_dimension=0, tiled=True
-    )
+    grad1 = jnp.sum(grad1.astype(F32), axis=0)
+    grad2 = both[head:]
     second_out = second_layer(second_pattern, hidden, second_weight)
     bias_all = lax.psum(bias_part.reshape(n_mp, local * side), ("mp", "dp"))
     bias_grad = lax.dynamic_index_in_dim(bias_all, lax.axis_index("mp"), 0, keepdims=False)
     return (
         second_out,
-        grad1.reshape(local, -1).astype(F32),
+        grad1.reshape(local, -1),
         grad2.reshape(local, -1).astype(F32),
         bias_grad,
     )

time: 273 us -> 253 us (0.927)
  waiting for transfers between devices: 64.7 us -> 42.1 us
  local copies, waits for them, and re-layouts: 33.4 us -> 27.6 us
  starting transfers between devices: 4.67 us -> 9.2 us
    reduce_scatter x3 -> x1, waiting for transfers between devices: 64.6 us -> 30.6 us  [body(): both = lax.psum_scatter(both, 'dp', scatter_dimension=0, tiled=True)[0]]
    all_to_all x0 -> x1, waiting for transfers between devices: none -> 11.4 us  [body(): lax.all_to_all(both[:head].reshape(n_mp, -1, side), 'mp', split_axis=0, c...]
    unnamed x34 -> x30, local copies, waits for them, and re-layouts: 26.3 us -> 20.6 us
    all_to_all x0 -> x1, starting transfers between devices: none -> 4.6 us  [body(): lax.all_to_all(both[:head].reshape(n_mp, -1, side), 'mp', split_axis=0, c...]
  transfers between devices with their start and end apart: 5 -> 4, of which waited for: 2 -> 2; matrix products, arithmetic and copies ran while one was open for 2% -> 3% of each run, Pallas kernels for 19% -> 15%
where the time goes in v2:
time: 253 us; the launch traced here: 252 us
  blocking collectives  78 us (31%)
  Pallas kernels  76 us (30%)
  waiting for transfers between devices  42.1 us (17%)
  local copies, waits for them, and re-layouts  27.6 us (11%)
  between operations  14.9 us (6%)
  starting transfers between devices  9.2 us (4%)
  other arithmetic  3.78 us (1%)
    psum x1, blocking collectives, body(): bias_all = lax.psum(bias_part.reshape(n_mp, local * side), ('mp', 'dp'))  39.7 us
    reduce_scatter x1, waiting for transfers between devices, body(): both = lax.psum_scatter(both, 'dp', scatter_dimension=0, tiled=True)[0]  30.6 us
    pallas_call x1, Pallas kernels, first_layer(): pl.pallas_call(first_kernel, out_shape=(jax.ShapeDtypeStruct((blocks, row...  23.3 us
    unnamed x30, local copies, waits for them, and re-layouts  20.6 us
    unnamed x1, blocking collectives  20.3 us
    pallas_call x1, Pallas kernels, hidden_term(): pl.pallas_call(term_kernel, out_shape=jax.ShapeDtypeStruct((all_blocks, r...  19.7 us
    all_gather x1, blocking collectives, body(): weight = lax.all_gather(mine, 'mp', axis=0, tiled=True)  18 us
    pallas_call x1, Pallas kernels, second_gradient(): pl.pallas_call(grad_kernel, out_shape=jax.ShapeDtypeStruct(both.shape, BF...  13.9 us
  transfers between devices with their start and end apart: 4, of which 2 were waited for; matrix products, arithmetic and copies ran while one was open for 3% of the time, Pallas kernels for 15%

profile of v2, /device:TPU:0, one launch (start us, length us, event | category | flops | bytes accessed | tf_op | source)
XLA Modules:
  0.0 251.6 jit_solution(7035382839548367609)
XLA Ops:
  7.2 0.0 copy-start
  7.2 0.0 all-gather.3.cloned.1.call-start
  7.2 1.2 copy-done
  8.4 18.0 %all_gather.14 = bf16[2048,128]{1,0:T(8,128)(2,1)} all-gather(bf16[512,128]{1,0:T(8,128)(2,1)S(1)} %constant_dynamic-slice_fusion), channel_id=1, replica_groups=mesh['dp'=8,'mp'=4] {'mp'}, dimensions={0}, use_global_device_ids=true | all-gather | bytes 655360 | tf_op jit(solution)/shard_map/all_gather | solution.py:269
  26.4 0.0 all-gather.3.cloned.1.call-update
  26.4 6.3 %pick.1 = bf16[8,128,1024]{2,1,0:T(8,128)(2,1)} custom-call(s32[8]{0:T(128)} %bitcast.18, bf16[32,128,1024]{2,1,0:T(8,128)(2,1)} %bitcast.16), custom_call_target="tpu_custom_call" | custom-call | tf_op jit(solution)/shard_map/pick/pallas_call | solution.py:32
  32.8 0.0 copy-start.9
  32.8 0.0 copy-start.4
  32.8 4.5 %all-to-all-start = ((bf16[8,128,1024]{2,1,0:T(8,128)(2,1)}), bf16[8,128,1024]{2,1,0:T(8,128)(2,1)}, u32[]{:S(2)}, u32[]{:S(2)}) async-start(bf16[8,128,1024]{2,1,0:T(8,128)(2,1)} %pick.1), calls=%async_computation | async-start | bytes 4194304 | tf_op jit(solution)/shard_map/all_to_all | solution.py:264
  37.3 0.0 reduce-scatter.2.cloned.1.call-start
  37.4 0.0 copy-done.12
  37.4 0.1 copy.16
  37.5 0.1 reshape.76
  37.6 0.6 dynamic-slice
  38.9 0.1 maximum_dynamic-update-slice_fusion
  39.0 20.3 %all-reduce = f32[8320]{0:T(1024)S(1)} all-reduce(f32[8320]{0:T(1024)S(1)} %maximum_dynamic-update-slice_fusion), channel_id=2, replica_groups=mesh['dp'=8,'mp'=4] {'mp'}, use_global_device_ids=true, to_apply=%add | all-reduce | flops 8320 | bytes 66560
  59.3 0.1 reshape.102
  59.4 0.1 reshape_reshape.7.bias
  59.5 0.1 reshape_reshape.6.pattern
  59.6 0.1 reshape.75.pattern
  59.6 0.2 reduce-window.9
  59.8 0.6 gather_fusion.1
  60.5 0.6 gather_fusion
  61.1 0.1 select_reduce_fusion.source
  61.3 19.7 %term.1.part = bf16[64,512,128]{2,1,0:T(8,128)(2,1)S(1)} custom-call(s32[256]{0:T(256)S(1)} %reshape.75.pattern, bf16[512,2048]{1,0:T(8,128)(2,1)S(1)} %copy-done.4, bf16[16,16,128,128]{3,2,1,0:T(8,128)(2,1)} %weight.3), custom_call_target="tpu_custom_call" | custom-call | flops 4294967296 | bytes 18874368 | tf_op jit(solution)/shard_map/term/pallas_call | solution.py:74
  81.0 3.2 %copy-done.7 = bf16[64,512,128]{2,1,0:T(8,128)(2,1)} copy-done((bf16[64,512,128]{2,1,0:T(8,128)(2,1)}, bf16[64,512,128]{2,1,0:T(8,128)(2,1)S(1)}, u32[]{:S(2)}) %copy-start.7) | copy-done | bytes 8388632
  84.1 0.0 all-to-all-done.got
  84.2 2.2 copy-done.8
  86.3 23.3 %first.1 = (bf16[64,512,128]{2,1,0:T(8,128)(2,1)S(1)}, bf16[64,128,512]{2,1,0:T(8,128)(2,1)}, bf16[8,6144,128]{2,1,0:T(8,128)(2,1)}, f32[64,1,128]{2,1,0:T(1,128)S(1)}) custom-call(s32[128]{0:T(128)S(1)} %reshape_reshape.6.pattern, s32[4]{0:T(128)S(1)} %select_reduce_fusion.source, bf16[8,128,1024]{2,1,0:T(8,128)(2,1)} %all-to-all-done.got, ...), custom_call_target="tpu_custom_call" | custom-call | flops 4294967296 | bytes 31457280 | tf_op jit(solution)/shard_map/first/pallas_call | solution.py:137
  109.7 3.2 %copy-done.5 = bf16[64,512,128]{2,1,0:T(8,128)(2,1)} copy-done((bf16[64,512,128]{2,1,0:T(8,128)(2,1)}, bf16[64,512,128]{2,1,0:T(8,128)(2,1)S(1)}, u32[]{:S(2)}) %copy-start.5) | copy-done | bytes 8388632
  112.9 3.4 %copy-done.3 = bf16[64,128,512]{2,1,0:T(8,128)(2,1)S(1)} copy-done((bf16[64,128,512]{2,1,0:T(8,128)(2,1)S(1)}, bf16[64,128,512]{2,1,0:T(8,128)(2,1)}, u32[]{:S(2)}) %copy-start.3) | copy-done | bytes 8388632
  116.3 13.9 %second_grad.1 = bf16[8,6144,128]{2,1,0:T(8,128)(2,1)} custom-call(s32[256]{0:T(256)S(1)} %reshape.75.pattern, bf16[64,128,512]{2,1,0:T(8,128)(2,1)S(1)} %copy-done.3, bf16[512,2048]{1,0:T(8,128)(2,1)S(1)} %copy-done.4, bf16[8,6144,128]{2,1,0:T(8,128)(2,1)} %get-tuple-element.10.both), custom_call_target="tpu_custom_call", output_to_operand_aliasing={{}: (3, {})} | custom-call | flops 4294967296 | bytes 18874368 | tf_op jit(solution)/shard_map/second_grad/pallas_call | solution.py:189
  130.2 0.0 reduce-scatter.2.cloned.1.call-update
  130.2 0.5 broadcast.63
  130.7 0.7 reduce.3
  131.5 39.7 %psum.7 = f32[4,2048]{1,0:T(4,128)S(1)} all-reduce(f32[4,2048]{1,0:T(4,128)S(1)} %reshape.84), channel_id=1, replica_groups=mesh['dp'=8,'mp'=4] {'mp','dp'}, use_global_device_ids=true, to_apply=%region_4.5 | all-reduce | flops 8192 | bytes 65536 | tf_op jit(solution)/shard_map/psum | solution.py:299
  171.1 0.6 constant_dynamic-slice_fusion.1
  171.7 3.4 %copy-done.2 = bf16[16,16,128,128]{3,2,1,0:T(8,128)(2,1)S(1)} copy-done((bf16[16,16,128,128]{3,2,1,0:T(8,128)(2,1)S(1)}, bf16[16,16,128,128]{3,2,1,0:T(8,128)(2,1)}, u32[]{:S(2)}) %copy-start.2) | copy-done | bytes 8388632
  175.1 3.4 %copy-done.6 = bf16[64,512,128]{2,1,0:T(8,128)(2,1)S(1)} copy-done((bf16[64,512,128]{2,1,0:T(8,128)(2,1)S(1)}, bf16[64,512,128]{2,1,0:T(8,128)(2,1)}, u32[]{:S(2)}) %copy-start.6) | copy-done | bytes 8388632
  178.5 12.8 %second_out.1 = bf16[512,2048]{1,0:T(8,128)(2,1)} custom-call(s32[256]{0:T(256)S(1)} %reshape.75.pattern, bf16[64,512,128]{2,1,0:T(8,128)(2,1)S(1)} %copy-done.6, bf16[16,16,128,128]{3,2,1,0:T(8,128)(2,1)S(1)} %copy-done.2), custom_call_target="tpu_custom_call" | custom-call | flops 4294967296 | bytes 18874368 | tf_op jit(solution)/shard_map/second_out/pallas_call | solution.py:221
  191.3 30.6 %reduce-scatter.2.cloned.1.call-done = bf16[1,6144,128]{2,1,0:T(8,128)(2,1)} async-done(((bf16[8,6144,128]{2,1,0:T(8,128)(2,1)}), bf16[1,6144,128]{2,1,0:T(8,128)(2,1)}) %reduce-scatter.2.cloned.1.call-update) | async-done | bytes 1572880 | tf_op jit(solution)/shard_map/reduce_scatter | solution.py:291
  221.9 1.9 slice.24
  223.8 4.6 %all-to-all-start.1 = ((bf16[4,512,128]{2,1,0:T(8,128)(2,1)}), bf16[4,512,128]{2,1,0:T(8,128)(2,1)}, u32[]{:S(2)}, u32[]{:S(2)}) async-start(bf16[4,512,128]{2,1,0:T(8,128)(2,1)} %bitcast.8), calls=%async_computation.2 | async-start | bytes 1048576 | tf_op jit(solution)/shard_map/all_to_all | solution.py:293
  228.4 1.4 slice_convert_fusion
  229.9 1.5 reshape.85
  231.4 11.4 %all-to-all-done.1 = bf16[4,512,128]{2,1,0:T(8,128)(2,1)} async-done(((bf16[4,512,128]{2,1,0:T(8,128)(2,1)}), bf16[4,512,128]{2,1,0:T(8,128)(2,1)}, u32[]{:S(2)}, u32[]{:S(2)}) %all-to-all-start.1) | async-done | bytes 524320 | tf_op jit(solution)/shard_map/all_to_all | solution.py:293
  242.8 1.1 convert_reduce_fusion
  244.0 0.8 reshape.83
  (28 shorter events, 0.1 us)
Async XLA Ops:
  7.2 1.2 copy-start
  7.2 77.0 %all-gather.3.cloned.1.call-start = ((), (), s32[]{:S(2)}) async-start(), calls=%async_computation.3 | async-start | bytes 4718592 | tf_op jit(solution)/shard_map/all_gather | solution.py:270
  32.8 4.6 %copy-start.12 = (s32[16,2]{0,1:T(2,128)S(1)}, s32[16,2]{0,1:T(2,128)}, u32[]{:S(2)}) copy-start(s32[16,2]{0,1:T(2,128)} %param.12) | copy-start | bytes 388
  32.8 4.8 %copy-start.13 = (u32[32]{0:T(128)S(1)}, u32[32]{0:T(128)}, u32[]{:S(2)}) copy-start(u32[32]{0:T(128)} %constant.57) | copy-start | bytes 388
  32.8 6.1 %copy-start.11 = (f32[2048]{0:T(1024)S(1)}, f32[2048]{0:T(1024)}, u32[]{:S(2)}) copy-start(f32[2048]{0:T(1024)} %param.14) | copy-start | bytes 24580
  32.8 26.8 %copy-start.10 = (s32[16,16]{1,0:T(8,128)S(1)}, s32[16,16]{1,0:T(8,128)}, u32[]{:S(2)}) copy-start(s32[16,16]{1,0:T(8,128)} %param.15) | copy-start | bytes 3076
  32.8 26.9 %copy-start.9 = (s32[1,8]{1,0:T(1,128)S(1)}, s32[1,8]{1,0:T(1,128)}, u32[]{:S(2)}) copy-start(s32[1,8]{1,0:T(1,128)} %param.11) | copy-start | bytes 100
  32.8 28.5 %copy-start.4 = (bf16[512,2048]{1,0:T(8,128)(2,1)S(1)}, bf16[512,2048]{1,0:T(8,128)(2,1)}, u32[]{:S(2)}) copy-start(bf16[512,2048]{1,0:T(8,128)(2,1)} %up.3) | copy-start | bytes 6291460
  32.8 51.3 %all-to-all-start = ((bf16[8,128,1024]{2,1,0:T(8,128)(2,1)}), bf16[8,128,1024]{2,1,0:T(8,128)(2,1)}, u32[]{:S(2)}, u32[]{:S(2)}) async-start(bf16[8,128,1024]{2,1,0:T(8,128)(2,1)} %pick.1), calls=%async_computation | async-start | bytes 4194304 | tf_op jit(solution)/shard_map/all_to_all | solution.py:264
  37.3 184.6 %reduce-scatter.2.cloned.1.call-start = ((), (), s32[]{:S(2)}) async-start(), calls=%async_computation.4 | async-start | bytes 14155776 | tf_op jit(solution)/shard_map/reduce_scatter | solution.py:291
  80.9 3.2 %copy-start.7 = (bf16[64,512,128]{2,1,0:T(8,128)(2,1)}, bf16[64,512,128]{2,1,0:T(8,128)(2,1)S(1)}, u32[]{:S(2)}) copy-start(bf16[64,512,128]{2,1,0:T(8,128)(2,1)S(1)} %term.1.part) | copy-start | bytes 25165828
  84.1 2.2 copy-start.8
  109.7 3.2 %copy-start.5 = (bf16[64,512,128]{2,1,0:T(8,128)(2,1)}, bf16[64,512,128]{2,1,0:T(8,128)(2,1)S(1)}, u32[]{:S(2)}) copy-start(bf16[64,512,128]{2,1,0:T(8,128)(2,1)S(1)} %get-tuple-element.8.hidden) | copy-start | bytes 25165828
  112.9 3.4 %copy-start.3 = (bf16[64,128,512]{2,1,0:T(8,128)(2,1)S(1)}, bf16[64,128,512]{2,1,0:T(8,128)(2,1)}, u32[]{:S(2)}) copy-start(bf16[64,128,512]{2,1,0:T(8,128)(2,1)} %get-tuple-element.9.hidden_t) | copy-start | bytes 25165828
  171.7 3.4 %copy-start.2 = (bf16[16,16,128,128]{3,2,1,0:T(8,128)(2,1)S(1)}, bf16[16,16,128,128]{3,2,1,0:T(8,128)(2,1)}, u32[]{:S(2)}) copy-start(bf16[16,16,128,128]{3,2,1,0:T(8,128)(2,1)} %weight.3) | copy-start | bytes 25165828
  175.1 3.4 %copy-start.6 = (bf16[64,512,128]{2,1,0:T(8,128)(2,1)S(1)}, bf16[64,512,128]{2,1,0:T(8,128)(2,1)}, u32[]{:S(2)}) copy-start(bf16[64,512,128]{2,1,0:T(8,128)(2,1)} %copy-done.5) | copy-start | bytes 25165828
  223.8 19.0 %all-to-all-start.1 = ((bf16[4,512,128]{2,1,0:T(8,128)(2,1)}), bf16[4,512,128]{2,1,0:T(8,128)(2,1)}, u32[]{:S(2)}, u32[]{:S(2)}) async-start(bf16[4,512,128]{2,1,0:T(8,128)(2,1)} %bitcast.8), calls=%async_computation.2 | async-start | bytes 1048576 | tf_op jit(solution)/shard_map/all_to_all | solution.py:293
  228.4 16.3 %copy-start.1 = (bf16[16,2,128,128]{3,2,1,0:T(8,128)(2,1)S(1)}, bf16[16,2,128,128]{3,2,1,0:T(8,128)(2,1)}, u32[]{:S(2)}) copy-start(bf16[16,2,128,128]{3,2,1,0:T(8,128)(2,1)} %param.13) | copy-start | bytes 3145732
Sparse Core Ops, SparseCore 0:
  26.6 54.2 all-gather.2
  130.3 91.5 reduce-scatter.1
